TPU v7x, 128 devices: a whole 4x4x4 slice. The times are simulated.
128 devices in a mesh: group: 4 (over z_lo, core), dp: 2 (over z_hi), tensor: 16 (over x, y).
Axes of the slice: x: 4, y: 4, z: 4 (z_hi: 2, z_lo: 2; z = z_hi * 2 + z_lo), core: 2. Of those that a mesh axis runs over, the one named last changes fastest.
Arguments:
- tokens: bfloat16 [2048, 8, 2048], P('tensor', ('group', 'dp')), may hold values from -6 to 6
- cotangent: bfloat16 [2048, 8, 2048], P('tensor', ('group', 'dp')), may hold values from -6 to 6
- lengths: int32 [8], replicated, may hold values from 1 to 2048, 9830 in all
- ln1_gain: float32 [2048], replicated, may hold values from 0.25 to 1.75
- ln1_bias: float32 [2048], replicated, may hold values from -1.75 to 1.75
- w_qkv: bfloat16 [2048, 3, 16, 128], P(None, None, 'tensor'), may hold values from -0.125 to 0.125
- b_qv: float32 [2, 2048], P(None, 'tensor'), may hold values from -1.75 to 1.75
- w_o: bfloat16 [16, 128, 2048], P('tensor'), may hold values from -0.75 to 0.75
- b_o: float32 [2048], replicated, may hold values from -1.75 to 1.75
- ln2_gain: float32 [2048], replicated, may hold values from 0.25 to 1.75
- ln2_bias: float32 [2048], replicated, may hold values from -1.75 to 1.75
- w_in: bfloat16 [2048, 8192], P(None, 'tensor'), may hold values from -0.125 to 0.125
- b_in: float32 [8192], P('tensor'), may hold values from -1.75 to 1.75
- w_out: bfloat16 [8192, 2048], P('tensor'), may hold values from -0.0625 to 0.0625
- b_out: float32 [2048], replicated, may hold values from -1.75 to 1.75
Outputs:
- output: bfloat16 [2048, 8, 2048], P('tensor', ('group', 'dp'))
- input_grad: bfloat16 [2048, 8, 2048], P('tensor', ('group', 'dp'))
- d_ln1_gain: float32 [2048], P(('group', 'dp', 'tensor'))
- d_ln1_bias: float32 [2048], P(('group', 'dp', 'tensor'))
- d_w_qkv: float32 [2048, 3, 16, 128], P(('group', 'dp'), None, 'tensor')
- d_b_qv: float32 [2, 2048], P(None, ('group', 'dp', 'tensor'))
- d_w_o: float32 [16, 128, 2048], P('tensor', None, ('group', 'dp'))
- d_b_o: float32 [2048], P(('group', 'dp', 'tensor'))
- d_ln2_gain: float32 [2048], P(('group', 'dp', 'tensor'))
- d_ln2_bias: float32 [2048], P(('group', 'dp', 'tensor'))
- d_w_in: float32 [2048, 8192], P(('group', 'dp'), 'tensor')
- d_b_in: float32 [8192], P(('group', 'dp', 'tensor'))
- d_w_out: float32 [8192, 2048], P('tensor', ('group', 'dp'))
- d_b_out: float32 [2048], P(('group', 'dp', 'tensor'))
Inputs may be any that keep to these rules, and one draw needn't show every extreme that they name: The true lengths of the 8 sequences sum to 9830.
All inputs are finite; a program needn't handle non-finite values.
Results may differ from a plain program's by a relative error of at most 0.02.
Values may be sent and summed in bfloat16 or wider, within the bound.
No kernel may reach another device: no remote copies, remote signals or barrier semaphores. Data moves between devices by JAX's collectives and lax.ppermute only.
A program may use at most 192 MiB of HBM per device.

v0:
```python
from functools import partial
import math
import jax
import jax.numpy as jnp
from jax import lax
from jax.sharding import PartitionSpec as P

EPS = 1e-05
NEGATIVE = -1e30


def layer_norm(value, gain, shift):
    mean = jnp.mean(value, axis=-1, keepdims=True)
    centred = value - mean
    spread = jnp.mean(centred * centred, axis=-1, keepdims=True)
    return centred * lax.rsqrt(spread + EPS) * gain + shift


def gelu_tanh(value):
    return jax.nn.gelu(value, approximate=True)


def block_scores(rows_query, key_rows, first, length, score_scale):
    count = rows_query.shape[0]
    key_pos = jnp.arange(key_rows.shape[0], dtype=jnp.int32)
    query_pos = first + jnp.arange(count, dtype=jnp.int32)
    valid = (key_pos[None, :] <= query_pos[:, None]) & (key_pos[None, :] < length)
    scores = (
        lax.dot_general(
            rows_query, key_rows, (((1,), (1,)), ((), ())), preferred_element_type=jnp.float32
        )
        * score_scale
    )
    return (jnp.where(valid, scores, NEGATIVE), valid)


def attend_forward(item, block_rows, score_scale):
    query, key_rows, value_rows, length = item
    outputs = []
    log_parts = []
    for first in range(0, query.shape[0], block_rows):
        rows_query = query[first : first + block_rows]
        scores, valid = block_scores(rows_query, key_rows, first, length, score_scale)
        peak = jnp.max(scores, axis=-1, keepdims=True)
        expo = jnp.exp(scores - peak)
        weight_sum = jnp.sum(expo, axis=-1, keepdims=True)
        probs = (expo / weight_sum).astype(jnp.bfloat16)
        outputs.append(
            jnp.dot(probs, value_rows, preferred_element_type=jnp.float32).astype(jnp.bfloat16)
        )
        log_parts.append((peak + jnp.log(weight_sum))[:, 0])
    return (jnp.concatenate(outputs, 0), jnp.concatenate(log_parts, 0))


def attend_backward(item, block_rows, score_scale):
    query, key_rows, value_rows, length, grad_out, log_sums = item
    key_grad = jnp.zeros(key_rows.shape, jnp.float32)
    value_grad = jnp.zeros(value_rows.shape, jnp.float32)
    query_parts = []
    for first in range(0, query.shape[0], block_rows):
        rows_query = query[first : first + block_rows]
        scores, valid = block_scores(rows_query, key_rows, first, length, score_scale)
        probs = jnp.where(valid, jnp.exp(scores - log_sums[first : first + block_rows, None]), 0.0)
        grad_rows = grad_out[first : first + block_rows]
        probs_grad = lax.dot_general(
            grad_rows, value_rows, (((1,), (1,)), ((), ())), preferred_element_type=jnp.float32
        )
        inner = jnp.sum(probs * probs_grad, axis=-1, keepdims=True)
        score_grad = (probs * (probs_grad - inner)).astype(jnp.bfloat16)
        query_parts.append(
            jnp.dot(score_grad, key_rows, preferred_element_type=jnp.float32) * score_scale
        )
        key_grad = (
            key_grad
            + lax.dot_general(
                score_grad, rows_query, (((0,), (0,)), ((), ())), preferred_element_type=jnp.float32
            )
            * score_scale
        )
        value_grad = value_grad + lax.dot_general(
            probs.astype(jnp.bfloat16),
            grad_rows,
            (((0,), (0,)), ((), ())),
            preferred_element_type=jnp.float32,
        )
    return (
        jnp.concatenate(query_parts, 0).astype(jnp.bfloat16),
        key_grad.astype(jnp.bfloat16),
        value_grad.astype(jnp.bfloat16),
    )


def shards(
    tokens,
    cotangent,
    lengths,
    ln1_gain,
    ln1_bias,
    w_qkv,
    b_qv,
    w_o,
    b_o,
    ln2_gain,
    ln2_bias,
    w_in,
    b_in,
    w_out,
    b_out,
):
    row_count, seq_count, model_width = tokens.shape
    tensor_count = lax.axis_size("tensor")
    tensor_rank = lax.axis_index("tensor")
    seq_total = row_count * tensor_count
    local_heads = w_qkv.shape[2]
    head_size = w_qkv.shape[3]
    local_width = local_heads * head_size
    hidden = w_in.shape[1]
    block_rows = min(512, seq_total)
    score_scale = 1.0 / math.sqrt(head_size)
    group_count = lax.axis_size("group")
    group_rank = lax.axis_index("group")
    member = group_rank * lax.axis_size("dp") + lax.axis_index("dp")
    seq_lengths = lax.dynamic_slice_in_dim(lengths, member * seq_count, seq_count, 0)
    group_totals = jnp.sum(lengths.reshape(group_count, -1), axis=1).astype(jnp.float32)
    factor = (
        group_count
        * lax.dynamic_index_in_dim(group_totals, group_rank, 0, keepdims=False)
        / jnp.sum(group_totals)
    )
    inputs = tokens.astype(jnp.float32)
    normed_low = layer_norm(inputs, ln1_gain, ln1_bias).astype(jnp.bfloat16)
    normed_full = lax.all_gather(normed_low, "tensor", axis=0, tiled=True)
    joint_weight = w_qkv.reshape(model_width, 3 * local_width)
    projected = jnp.dot(
        normed_full.reshape(seq_total * seq_count, model_width),
        joint_weight,
        preferred_element_type=jnp.float32,
    )
    projected = projected.reshape(seq_total, seq_count, 3, local_width)
    query = (projected[:, :, 0] + b_qv[0]).astype(jnp.bfloat16)
    keys = projected[:, :, 1].astype(jnp.bfloat16)
    values = (projected[:, :, 2] + b_qv[1]).astype(jnp.bfloat16)

    def per_item(array):
        shaped = array.reshape(seq_total, seq_count, local_heads, head_size)
        return jnp.transpose(shaped, (1, 2, 0, 3)).reshape(
            seq_count * local_heads, seq_total, head_size
        )

    def per_row(array):
        shaped = array.reshape(seq_count, local_heads, seq_total, head_size)
        return jnp.transpose(shaped, (2, 0, 1, 3)).reshape(seq_total, seq_count, local_width)

    query_items = per_item(query)
    key_items = per_item(keys)
    value_items = per_item(values)
    item_lengths = jnp.repeat(seq_lengths, local_heads)
    heads_out, log_sums = lax.map(
        partial(attend_forward, block_rows=block_rows, score_scale=score_scale),
        (query_items, key_items, value_items, item_lengths),
    )
    attended = per_row(heads_out)
    out_weight = w_o.reshape(local_width, model_width)
    piece = attended
    attention = (
        lax.psum_scatter(
            jnp.einsum("rse,ed->rsd", piece, out_weight, preferred_element_type=jnp.float32),
            "tensor",
            scatter_dimension=0,
            tiled=True,
        )
        + b_o
    )
    middle = inputs + attention
    second_low = layer_norm(middle, ln2_gain, ln2_bias).astype(jnp.bfloat16)
    second_full = lax.all_gather(second_low, "tensor", axis=0, tiled=True)
    pre_act = (
        jnp.dot(
            second_full.reshape(seq_total * seq_count, model_width),
            w_in,
            preferred_element_type=jnp.float32,
        )
        + b_in
    )
    activated = gelu_tanh(pre_act).astype(jnp.bfloat16).reshape(seq_total, seq_count, hidden)
    piece = activated
    feed = (
        lax.psum_scatter(
            jnp.einsum("rsf,fd->rsd", piece, w_out, preferred_element_type=jnp.float32).astype(
                jnp.bfloat16
            ),
            "tensor",
            scatter_dimension=0,
            tiled=True,
        ).astype(jnp.float32)
        + b_out
    )
    output = (middle + feed).astype(jnp.bfloat16)
    positions = tensor_rank * row_count + jnp.arange(row_count, dtype=jnp.int32)
    live = positions[:, None] < seq_lengths[None, :]
    upstream = jnp.where(live[:, :, None], cotangent, jnp.zeros_like(cotangent))
    piece = lax.all_gather(upstream, "tensor", axis=0, tiled=True)
    weight_grad = jnp.einsum("rsf,rsd->fd", activated, piece, preferred_element_type=jnp.float32)
    part = jnp.einsum("rsd,fd->rsf", piece, w_out, preferred_element_type=jnp.float32)
    act_grad = part
    grad_w_out = weight_grad
    gelu_back = jax.vjp(gelu_tanh, pre_act)[1]
    pre_low = gelu_back(act_grad.reshape(seq_total * seq_count, hidden))[0].astype(jnp.bfloat16)
    grad_b_in = jnp.sum(pre_low, axis=0, dtype=jnp.float32)
    grad_w_in = jnp.einsum(
        "rd,rf->df",
        second_full.reshape(seq_total * seq_count, model_width),
        pre_low,
        preferred_element_type=jnp.float32,
    )
    pre_rows = pre_low.reshape(seq_total, seq_count, hidden)
    piece = pre_rows
    second_grad = lax.psum_scatter(
        jnp.einsum("rsf,df->rsd", piece, w_in, preferred_element_type=jnp.float32),
        "tensor",
        scatter_dimension=0,
        tiled=True,
    )
    norm_two_back = jax.vjp(layer_norm, middle, ln2_gain, ln2_bias)[1]
    middle_part, grad_ln2_gain, grad_ln2_bias = norm_two_back(second_grad)
    middle_grad = upstream.astype(jnp.float32) + middle_part
    branch_low = middle_grad.astype(jnp.bfloat16)
    grad_b_o = jnp.sum(branch_low, axis=(0, 1), dtype=jnp.float32)
    grad_b_out = jnp.sum(upstream, axis=(0, 1), dtype=jnp.float32)
    piece = lax.all_gather(branch_low, "tensor", axis=0, tiled=True)
    weight_grad = jnp.einsum("rse,rsd->ed", attended, piece, preferred_element_type=jnp.float32)
    part = jnp.einsum("rsd,ed->rse", piece, out_weight, preferred_element_type=jnp.float32)
    head_items = per_item(part.astype(jnp.bfloat16))
    grads_query, grads_keys, grads_values = lax.map(
        partial(attend_backward, block_rows=block_rows, score_scale=score_scale),
        (query_items, key_items, value_items, item_lengths, head_items, log_sums),
    )
    joint_grad = jnp.stack(
        (per_row(grads_query), per_row(grads_keys), per_row(grads_values)), axis=2
    )
    grad_b_qv = jnp.sum(joint_grad[:, :, 0::2], axis=(0, 1), dtype=jnp.float32)
    joint_rows = joint_grad.reshape(seq_total, seq_count, 3 * local_width)
    grad_w_qkv = jnp.einsum(
        "rd,rc->dc",
        normed_full.reshape(seq_total * seq_count, model_width),
        joint_rows.reshape(seq_total * seq_count, 3 * local_width),
        preferred_element_type=jnp.float32,
    )
    piece = joint_rows
    normed_grad = lax.psum_scatter(
        jnp.einsum("rsc,dc->rsd", piece, joint_weight, preferred_element_type=jnp.float32).astype(
            jnp.bfloat16
        ),
        "tensor",
        scatter_dimension=0,
        tiled=True,
    ).astype(jnp.float32)
    norm_one_back = jax.vjp(layer_norm, inputs, ln1_gain, ln1_bias)[1]
    input_part, grad_ln1_gain, grad_ln1_bias = norm_one_back(normed_grad)
    input_grad = (middle_grad + input_part).astype(jnp.bfloat16)
    matrices = (
        grad_w_qkv.reshape(model_width, 3, local_heads, head_size) * factor,
        weight_grad.reshape(local_heads, head_size, model_width) * factor,
        grad_w_in * factor,
        grad_w_out * factor,
    )
    summed = (
        lax.psum_scatter(
            matrices[0].astype(jnp.bfloat16), ("group", "dp"), scatter_dimension=0, tiled=True
        ).astype(jnp.float32),
        lax.psum_scatter(
            matrices[1].astype(jnp.bfloat16), ("group", "dp"), scatter_dimension=2, tiled=True
        ).astype(jnp.float32),
        lax.psum_scatter(
            matrices[2].astype(jnp.bfloat16), ("group", "dp"), scatter_dimension=0, tiled=True
        ).astype(jnp.float32),
        lax.psum_scatter(
            matrices[3].astype(jnp.bfloat16), ("group", "dp"), scatter_dimension=1, tiled=True
        ).astype(jnp.float32),
    )
    in_full = lax.dynamic_update_slice_in_dim(
        jnp.zeros((hidden * tensor_count,), jnp.float32), grad_b_in, tensor_rank * hidden, 0
    )
    joint_full = lax.dynamic_update_slice_in_dim(
        jnp.zeros((2, local_width * tensor_count), jnp.float32),
        grad_b_qv,
        tensor_rank * local_width,
        1,
    )
    stacked = (
        jnp.concatenate(
            (
                jnp.stack(
                    (
                        grad_ln1_gain,
                        grad_ln1_bias,
                        grad_b_o,
                        grad_ln2_gain,
                        grad_ln2_bias,
                        grad_b_out,
                    )
                ),
                joint_full,
            ),
            0,
        )
        * factor
    )
    vector_sums, in_sums = (
        lax.psum_scatter(stacked, ("group", "dp", "tensor"), scatter_dimension=1, tiled=True),
        lax.psum_scatter(
            in_full * factor, ("group", "dp", "tensor"), scatter_dimension=0, tiled=True
        ),
    )
    return (
        output,
        input_grad,
        vector_sums[0],
        vector_sums[1],
        summed[0],
        vector_sums[6:8],
        summed[1],
        vector_sums[2],
        vector_sums[3],
        vector_sums[4],
        summed[2],
        in_sums,
        summed[3],
        vector_sums[5],
    )


def solution(mesh):
    in_specs = (
        P("tensor", ("group", "dp"), None),
        P("tensor", ("group", "dp"), None),
        P(),
        P(),
        P(),
        P(None, None, "tensor", None),
        P(None, "tensor"),
        P("tensor", None, None),
        P(),
        P(),
        P(),
        P(None, "tensor"),
        P("tensor"),
        P("tensor", None),
        P(),
    )
    out_specs = (
        P("tensor", ("group", "dp"), None),
        P("tensor", ("group", "dp"), None),
        P(("group", "dp", "tensor")),
        P(("group", "dp", "tensor")),
        P(("group", "dp"), None, "tensor", None),
        P(None, ("group", "dp", "tensor")),
        P("tensor", None, ("group", "dp")),
        P(("group", "dp", "tensor")),
        P(("group", "dp", "tensor")),
        P(("group", "dp", "tensor")),
        P(("group", "dp"), "tensor"),
        P(("group", "dp", "tensor")),
        P("tensor", ("group", "dp")),
        P(("group", "dp", "tensor")),
    )
    return jax.shard_map(shards, mesh=mesh, in_specs=in_specs, out_specs=out_specs, check_vma=False)
```

profile of v0, /device:TPU:96, one launch (start us, length us, event | category | flops | bytes accessed | tf_op | source)
XLA Modules:
  0.0 1723.6 jit_solution(11324964571885417214)
XLA Ops:
  16.8 68.1 %all-gather.5.cloned.1.call-done = bf16[2048,1,2048]{2,0,1:T(8,128)(2,1)} async-done(((bf16[128,1,2048]{2,0,1:T(8,128)(2,1)}), bf16[2048,1,2048]{2,0,1:T(8,128)(2,1)}) %all-gather.5.cloned.1.call-update) | async-done | bytes 8388624 | tf_op jit(solution)/shard_map/all_gather | solution.py:132
  84.8 7.4 fusion.31
  97.1 3.9 fusion.116
  101.0 4.0 online-softmax.3
  106.0 5.1 fusion.115
  111.1 4.0 online-softmax.2
  116.1 5.1 fusion.114
  121.1 4.0 online-softmax.1
  126.2 4.4 online-softmax
  132.2 8.1 convolution_bitcast_fusion.1
  140.4 110.3 %reduce-scatter.12.cloned.1.call-done = f32[128,1,2048]{2,0,1:T(8,128)} async-done(((f32[2048,1,2048]{2,0,1:T(8,128)}), f32[128,1,2048]{2,0,1:T(8,128)}) %reduce-scatter.12.cloned.1.call-update) | async-done | bytes 1048592 | tf_op jit(solution)/shard_map/reduce_scatter | solution.py:166
  258.8 67.0 %all-gather.7.cloned.1.call-done = bf16[2048,1,2048]{2,0,1:T(8,128)(2,1)} async-done(((bf16[128,1,2048]{2,0,1:T(8,128)(2,1)}), bf16[2048,1,2048]{2,0,1:T(8,128)(2,1)}) %all-gather.7.cloned.1.call-update) | async-done | bytes 8388624 | tf_op jit(solution)/shard_map/all_gather | solution.py:176
  325.7 10.5 fusion.10
  336.2 62.4 %all-gather.9.cloned.1.call-done = bf16[2048,1,2048]{2,0,1:T(8,128)(2,1)} async-done(((bf16[128,1,2048]{2,0,1:T(8,128)(2,1)}), bf16[2048,1,2048]{2,0,1:T(8,128)(2,1)}) %all-gather.9.cloned.1.call-update) | async-done | bytes 8388624 | tf_op jit(solution)/shard_map/all_gather | solution.py:202
  398.7 12.4 convert_reduce_fusion
  412.5 8.2 convolution_bitcast_fusion
  420.8 10.3 convert_bitcast_fusion.1
  431.2 99.9 %reduce-scatter.16.cloned.1.call-done = f32[128,1,2048]{2,0,1:T(8,128)} async-done(((f32[2048,1,2048]{2,0,1:T(8,128)}), f32[128,1,2048]{2,0,1:T(8,128)}) %reduce-scatter.16.cloned.1.call-update) | async-done | bytes 1048592 | tf_op jit(solution)/shard_map/reduce_scatter | solution.py:218
  533.3 85.7 %reduce-scatter.14.cloned.1.call-done = bf16[128,1,2048]{2,0,1:T(8,128)(2,1)} async-done(((bf16[2048,1,2048]{2,0,1:T(8,128)(2,1)}), bf16[128,1,2048]{2,0,1:T(8,128)(2,1)}) %reduce-scatter.14.cloned.1.call-update) | async-done | bytes 524304 | tf_op jit(solution)/shard_map/reduce_scatter | solution.py:188
  625.8 11.3 multiply_convert_fusion
  645.5 9.6 multiply_convert_fusion.1
  655.6 37.3 %all-gather.11.cloned.1.call-done = bf16[2048,1,2048]{2,0,1:T(8,128)(2,1)} async-done(((bf16[128,1,2048]{2,0,1:T(8,128)(2,1)}), bf16[2048,1,2048]{2,0,1:T(8,128)(2,1)}) %all-gather.11.cloned.1.call-update) | async-done | bytes 8388624 | tf_op jit(solution)/shard_map/all_gather | solution.py:230
  692.9 5.9 fusion.45
  708.0 9.5 multiply_reduce_fusion
  717.5 4.5 multiply_convert_fusion.3
  722.1 9.5 multiply_convert_fusion.2
  755.2 8.3 fusion.38
  763.6 9.7 convert_bitcast_fusion
  774.1 75.9 %all-reduce = f32[8192]{0:T(1024)S(1)} all-reduce(f32[8192]{0:T(1024)S(1)} %broadcast_multiply_fusion.1), channel_id=10, replica_groups=mesh['group'=4,'dp'=2,'tensor'=16] {'group','dp','tensor'}, use_global_device_ids=true, to_apply=%region_38.39.clone | all-reduce | flops 8192 | bytes 65536
  857.0 45.5 %reduce-scatter.20.cloned.1.call-done = bf16[256,3,1,128]{3,0,1,2:T(8,128)(2,1)} async-done(((bf16[2048,3,1,128]{3,0,1,2:T(8,128)(2,1)}), bf16[256,3,1,128]{3,0,1,2:T(8,128)(2,1)}) %reduce-scatter.20.cloned.1.call-update) | async-done | bytes 196624 | tf_op jit(solution)/shard_map/reduce_scatter | solution.py:268
  904.5 90.2 %reduce-scatter.18.cloned.1.call-done = bf16[128,1,2048]{2,0,1:T(8,128)(2,1)} async-done(((bf16[2048,1,2048]{2,0,1:T(8,128)(2,1)}), bf16[128,1,2048]{2,0,1:T(8,128)(2,1)}) %reduce-scatter.18.cloned.1.call-update) | async-done | bytes 524304 | tf_op jit(solution)/shard_map/reduce_scatter | solution.py:250
  1002.0 709.0 %reduce-scatter.28.cloned.1.call-done = f32[16,8]{1,0:T(8,128)} async-done(((f32[2048,8]{1,0:T(8,128)}), f32[16,8]{1,0:T(8,128)}) %reduce-scatter.28.cloned.1.call-update) | async-done | bytes 528
  (271 shorter events, 100.3 us)
Async XLA Ops:
  7.2 391.5 %copy-start = (bf16[512,2048]{1,0:T(8,128)(2,1)S(1)}, bf16[512,2048]{1,0:T(8,128)(2,1)}, u32[]{:S(2)}) copy-start(bf16[512,2048]{1,0:T(8,128)(2,1)} %param.28) | copy-start | bytes 6291460
  7.2 77.6 %all-gather.5.cloned.1.call-start = ((), (), s32[]{:S(2)}) async-start(), calls=%async_computation.9 | async-start | bytes 8912896 | tf_op jit(solution)/shard_map/all_gather | solution.py:132
  12.8 237.9 %reduce-scatter.12.cloned.1.call-start = ((), (), s32[]{:S(2)}) async-start(), calls=%async_computation.10 | async-start | bytes 17825792 | tf_op jit(solution)/shard_map/reduce_scatter | solution.py:166
  140.3 113.3 %copy-start.29 = (f32[2048]{0:T(1024)S(1)}, f32[2048]{0:T(1024)}, u32[]{:S(2)}) copy-start(f32[2048]{0:T(1024)} %param.24) | copy-start | bytes 24580
  140.3 185.4 %all-gather.7.cloned.1.call-start = ((), (), s32[]{:S(2)}) async-start(), calls=%async_computation.11 | async-start | bytes 8912896 | tf_op jit(solution)/shard_map/all_gather | solution.py:176
  255.3 143.3 %all-gather.9.cloned.1.call-start = ((), (), s32[]{:S(2)}) async-start(), calls=%async_computation.13 | async-start | bytes 8912896 | tf_op jit(solution)/shard_map/all_gather | solution.py:202
  258.7 272.4 %reduce-scatter.16.cloned.1.call-start = ((), (), s32[]{:S(2)}) async-start(), calls=%async_computation.14 | async-start | bytes 17825792 | tf_op jit(solution)/shard_map/reduce_scatter | solution.py:218
  420.7 198.3 %reduce-scatter.14.cloned.1.call-start = ((), (), s32[]{:S(2)}) async-start(), calls=%async_computation.12 | async-start | bytes 8912896 | tf_op jit(solution)/shard_map/reduce_scatter | solution.py:188
  431.0 100.0 %copy-start.59 = (f32[128]{0:T(128)S(1)}, f32[128]{0:T(128)}, u32[]{:S(2)}) copy-start(f32[128]{0:T(128)} %copy-done.58) | copy-start | bytes 1540
  431.0 102.2 %copy-start.65 = (f32[128]{0:T(128)S(1)}, f32[128]{0:T(128)}, u32[]{:S(2)}) copy-start(f32[128]{0:T(128)} %copy-done.64) | copy-start | bytes 1540
  431.0 188.0 %copy-start.51 = (f32[2048]{0:T(1024)S(1)}, f32[2048]{0:T(1024)}, u32[]{:S(2)}) copy-start(f32[2048]{0:T(1024)} %param.29) | copy-start | bytes 24580
  431.1 190.5 %copy-start.15 = (bf16[128,1,2048]{2,0,1:T(8,128)(2,1)S(1)}, bf16[128,1,2048]{2,0,1:T(8,128)(2,1)}, u32[]{:S(2)}) copy-start(bf16[128,1,2048]{2,0,1:T(8,128)(2,1)} %get-tuple-element.119) | copy-start | bytes 1572868
  431.1 191.9 %copy-start.67 = (s32[8]{0:T(128)S(1)}, s32[8]{0:T(128)}, u32[]{:S(2)}) copy-start(s32[8]{0:T(128)} %param.17) | copy-start | bytes 100
  431.1 194.6 %copy-start.71 = (f32[512]{0:T(512)S(1)}, f32[512]{0:T(512)}, u32[]{:S(2)}) copy-start(f32[512]{0:T(512)} %param.27) | copy-start | bytes 6148
  431.1 261.8 %all-gather.11.cloned.1.call-start = ((), (), s32[]{:S(2)}) async-start(), calls=%async_computation.15 | async-start | bytes 8912896 | tf_op jit(solution)/shard_map/all_gather | solution.py:230
  622.7 227.9 %reduce-scatter.26.cloned.1.call-start = ((), (), s32[]{:S(2)}) async-start(), calls=%async_computation.20 | async-start | bytes 2359296 | tf_op jit(solution)/shard_map/reduce_scatter | solution.py:277
  637.1 215.3 %reduce-scatter.24.cloned.1.call-start = ((), (), s32[]{:S(2)}) async-start(), calls=%async_computation.19 | async-start | bytes 2359296 | tf_op jit(solution)/shard_map/reduce_scatter | solution.py:274
  655.2 200.2 %reduce-scatter.22.cloned.1.call-start = ((), (), s32[]{:S(2)}) async-start(), calls=%async_computation.18 | async-start | bytes 589824 | tf_op jit(solution)/shard_map/reduce_scatter | solution.py:271
  752.4 150.2 %reduce-scatter.20.cloned.1.call-start = ((), (), s32[]{:S(2)}) async-start(), calls=%async_computation.17 | async-start | bytes 1769472 | tf_op jit(solution)/shard_map/reduce_scatter | solution.py:268
  763.6 231.1 %reduce-scatter.18.cloned.1.call-start = ((), (), s32[]{:S(2)}) async-start(), calls=%async_computation.16 | async-start | bytes 8912896 | tf_op jit(solution)/shard_map/reduce_scatter | solution.py:250
  773.3 221.4 %copy-start.9 = (bf16[128,1,2048]{2,0,1:T(8,128)(2,1)S(1)}, bf16[128,1,2048]{2,0,1:T(8,128)(2,1)}, u32[]{:S(2)}) copy-start(bf16[128,1,2048]{2,0,1:T(8,128)(2,1)} %param.15) | copy-start | bytes 1572868
  773.3 221.4 %copy-start.28 = (f32[2048]{0:T(1024)S(1)}, f32[2048]{0:T(1024)}, u32[]{:S(2)}) copy-start(f32[2048]{0:T(1024)} %param.18) | copy-start | bytes 24580
  773.3 221.4 %copy-start.46 = (f32[128]{0:T(128)S(1)}, f32[128]{0:T(128)}, u32[]{:S(2)}) copy-start(f32[128]{0:T(128)} %copy-done.45) | copy-start | bytes 1540
  773.3 222.8 %copy-start.69 = (f32[128]{0:T(128)S(1)}, f32[128]{0:T(128)}, u32[]{:S(2)}) copy-start(f32[128]{0:T(128)} %copy-done.68) | copy-start | bytes 1540
  773.3 222.8 %copy-start.55 = (f32[128]{0:T(128)S(1)}, f32[128]{0:T(128)}, u32[]{:S(2)}) copy-start(f32[128]{0:T(128)} %copy-done.54) | copy-start | bytes 1540
  773.3 224.4 %copy-start.30 = (f32[2048]{0:T(1024)S(1)}, f32[2048]{0:T(1024)}, u32[]{:S(2)}) copy-start(f32[2048]{0:T(1024)} %get-tuple-element.118) | copy-start | bytes 24580
  773.3 224.4 %copy-start.31 = (f32[2048]{0:T(1024)S(1)}, f32[2048]{0:T(1024)}, u32[]{:S(2)}) copy-start(f32[2048]{0:T(1024)} %get-tuple-element.107) | copy-start | bytes 24580
  773.4 224.4 %copy-start.32 = (f32[2048]{0:T(1024)S(1)}, f32[2048]{0:T(1024)}, u32[]{:S(2)}) copy-start(f32[2048]{0:T(1024)} %get-tuple-element.111) | copy-start | bytes 24580
  773.4 225.9 %copy-start.16 = (bf16[128,1,2048]{2,0,1:T(8,128)(2,1)S(1)}, bf16[128,1,2048]{2,0,1:T(8,128)(2,1)}, u32[]{:S(2)}) copy-start(bf16[128,1,2048]{2,0,1:T(8,128)(2,1)} %get-tuple-element.119) | copy-start | bytes 1572868
  773.4 225.9 %copy-start.61 = (f32[128]{0:T(128)S(1)}, f32[128]{0:T(128)}, u32[]{:S(2)}) copy-start(f32[128]{0:T(128)} %copy-done.60) | copy-start | bytes 1540
  773.4 937.6 %reduce-scatter.28.cloned.1.call-start = ((), (), s32[]{:S(2)}) async-start(), calls=%async_computation.21 | async-start | bytes 1056768
  855.4 861.5 %copy-start.1 = (bf16[512,2048]{1,0:T(8,128)(2,1)S(1)}, bf16[512,2048]{1,0:T(8,128)(2,1)}, u32[]{:S(2)}) copy-start(bf16[512,2048]{1,0:T(8,128)(2,1)} %param.28) | copy-start | bytes 6291460
  (57 other events, 1052.4 us)
Sparse Core Ops, SparseCore 0:
  12.9 71.8 all-gather.4
  140.5 110.1 reduce-scatter.11
  255.5 70.2 all-gather.6
  328.3 70.3 all-gather.8
  420.8 110.1 reduce-scatter.15
  534.3 84.6 reduce-scatter.13
  622.8 70.0 all-gather.10
  695.3 56.2 reduce-scatter.25
  754.1 60.7 reduce-scatter.23
  817.0 38.2 reduce-scatter.21
  857.9 44.5 reduce-scatter.19
  906.2 88.4 reduce-scatter.17
  999.3 711.5 reduce-scatter.27
where the time goes:
time: 1730 us; the launch traced here: 1720 us
  waiting for transfers between devices  1380 us (80%)
  matrix products  158 us (9%)
  blocking collectives  75.9 us (4%)
  other arithmetic  57.2 us (3%)
  local copies, waits for them, and re-layouts  22.4 us (1%)
    unnamed x14, waiting for transfers between devices  709 us
    reduce_scatter x1, waiting for transfers between devices, shards(): lax.psum_scatter(jnp.einsum('rse,ed->rsd', piece, out_weight, preferred_e...  110 us
    reduce_scatter x1, waiting for transfers between devices, shards(): lax.psum_scatter(jnp.einsum('rsf,df->rsd', piece, w_in, preferred_element...  99.9 us
    reduce_scatter x1, waiting for transfers between devices, shards(): lax.psum_scatter(jnp.einsum('rsc,dc->rsd', piece, joint_weight, preferred...  90.2 us
    reduce_scatter x1, waiting for transfers between devices, shards(): lax.psum_scatter(jnp.einsum('rsf,fd->rsd', piece, w_out, preferred_elemen...  85.7 us
    unnamed x1, blocking collectives  75.9 us
    all_gather x1, waiting for transfers between devices, shards(): normed_full = lax.all_gather(normed_low, 'tensor', axis=0, tiled=True)  68.1 us
    all_gather x1, waiting for transfers between devices, shards(): second_full = lax.all_gather(second_low, 'tensor', axis=0, tiled=True)  67 us
  transfers between devices with their start and end apart: 13, of which 11 were waited for; matrix products, arithmetic and copies ran while one was open for 9% of the time, Pallas kernels for 0%

commit v1 on v0

--- a/solution.py
+++ b/solution.py
@@ -7,6 +7,15 @@
 
 EPS = 1e-05
 NEGATIVE = -1e30
+recast_array = lambda message, axis_k: jnp.concatenate(
+    jax.lax.all_to_all(
+        jnp.stack([message] * jax.lax.axis_size("tensor")),
+        axis_name="tensor",
+        split_axis=0,
+        concat_axis=0,
+    ),
+    axis=axis_k,
+)
 
 
 def layer_norm(value, gain, shift):
@@ -199,7 +208,7 @@
     positions = tensor_rank * row_count + jnp.arange(row_count, dtype=jnp.int32)
     live = positions[:, None] < seq_lengths[None, :]
     upstream = jnp.where(live[:, :, None], cotangent, jnp.zeros_like(cotangent))
-    piece = lax.all_gather(upstream, "tensor", axis=0, tiled=True)
+    piece = recast_array(upstream, 0)
     weight_grad = jnp.einsum("rsf,rsd->fd", activated, piece, preferred_element_type=jnp.float32)
     part = jnp.einsum("rsd,fd->rsf", piece, w_out, preferred_element_type=jnp.float32)
     act_grad = part

time: 1730 us -> 1840 us (1.064)
  waiting for transfers between devices: 1380 us -> 1470 us
    all_gather x1, waiting for transfers between devices: 67 us -> 172 us  [shards(): second_full = lax.all_gather(second_low, 'tensor', axis=0, tiled=True)]
    all_gather x1 -> x0, waiting for transfers between devices: 62.4 us -> none  [shards(): piece = lax.all_gather(upstream, 'tensor', axis=0, tiled=True)]
    reduce_scatter x1, waiting for transfers between devices: 90.2 us -> 45 us  [shards(): lax.psum_scatter(jnp.einsum('rsc,dc->rsd', piece, joint_weight, preferred...]
    reduce_scatter x1, waiting for transfers between devices: 0.86 us -> 38.7 us  [shards(): lax.psum_scatter(matrices[1].astype(jnp.bfloat16), ('group', 'dp'), scatt...]
    reduce_scatter x1, waiting for transfers between devices: 0.01 us -> 27.6 us  [shards(): lax.psum_scatter(matrices[2].astype(jnp.bfloat16), ('group', 'dp'), scatt...]
    all_gather x1, waiting for transfers between devices: 37.3 us -> 61.5 us  [shards(): piece = lax.all_gather(branch_low, 'tensor', axis=0, tiled=True)]
    unnamed x14 -> x13, waiting for transfers between devices: 709 us -> 716 us
  transfers between devices with their start and end apart: 13 -> 13, of which waited for: 11 -> 11; matrix products, arithmetic and copies ran while one was open for 9% -> 5% of each run, Pallas kernels for 0% -> 0%
where the time goes in v1:
time: 1840 us; the launch traced here: 1830 us
  waiting for transfers between devices  1470 us (80%)
  matrix products  156 us (8%)
  blocking collectives  84.3 us (5%)
  other arithmetic  51.6 us (3%)
  local copies, waits for them, and re-layouts  25.8 us (1%)
    unnamed x13, waiting for transfers between devices  716 us
    all_gather x1, waiting for transfers between devices, shards(): second_full = lax.all_gather(second_low, 'tensor', axis=0, tiled=True)  172 us
    reduce_scatter x1, waiting for transfers between devices, shards(): lax.psum_scatter(jnp.einsum('rse,ed->rsd', piece, out_weight, preferred_e...  110 us
    reduce_scatter x1, waiting for transfers between devices, shards(): lax.psum_scatter(jnp.einsum('rsf,df->rsd', piece, w_in, preferred_element...  103 us
    reduce_scatter x1, waiting for transfers between devices, shards(): lax.psum_scatter(jnp.einsum('rsf,fd->rsd', piece, w_out, preferred_elemen...  86.3 us
    unnamed x1, blocking collectives  84.3 us
    all_gather x1, waiting for transfers between devices, shards(): normed_full = lax.all_gather(normed_low, 'tensor', axis=0, tiled=True)  68.1 us
    all_gather x1, waiting for transfers between devices, shards(): piece = lax.all_gather(branch_low, 'tensor', axis=0, tiled=True)  61.5 us
  transfers between devices with their start and end apart: 13, of which 11 were waited for; matrix products, arithmetic and copies ran while one was open for 5% of the time, Pallas kernels for 0%

profile of v1, /device:TPU:96, one launch (start us, length us, event | category | flops | bytes accessed | tf_op | source)
XLA Modules:
  0.0 1831.3 jit_solution(7939760736498513858)
XLA Ops:
  16.7 68.1 %all-gather.4.cloned.1.call-done = bf16[2048,1,2048]{2,0,1:T(8,128)(2,1)} async-done(((bf16[128,1,2048]{2,0,1:T(8,128)(2,1)}), bf16[2048,1,2048]{2,0,1:T(8,128)(2,1)}) %all-gather.4.cloned.1.call-update) | async-done | bytes 8388624 | tf_op jit(solution)/shard_map/all_gather | solution.py:141
  84.8 7.4 fusion.25
  99.8 4.1 online-softmax.3
  104.8 4.5 fusion.109
  114.3 4.6 fusion.108
  123.9 4.2 online-softmax
  129.2 8.0 convolution_bitcast_fusion.1
  137.3 110.2 %reduce-scatter.12.cloned.1.call-done = f32[128,1,2048]{2,0,1:T(8,128)} async-done(((f32[2048,1,2048]{2,0,1:T(8,128)}), f32[128,1,2048]{2,0,1:T(8,128)}) %reduce-scatter.12.cloned.1.call-update) | async-done | bytes 1048592 | tf_op jit(solution)/shard_map/reduce_scatter | solution.py:175
  252.3 4.3 stack.16
  256.6 5.2 all-to-all-start
  261.9 171.9 %all-gather.6.cloned.1.call-done = bf16[2048,1,2048]{2,0,1:T(8,128)(2,1)} async-done(((bf16[128,1,2048]{2,0,1:T(8,128)(2,1)}), bf16[2048,1,2048]{2,0,1:T(8,128)(2,1)}) %all-gather.6.cloned.1.call-update) | async-done | bytes 8388624 | tf_op jit(solution)/shard_map/all_gather | solution.py:185
  433.8 10.5 fusion.6
  444.4 12.4 convert_reduce_fusion
  458.2 8.3 convolution_bitcast_fusion
  466.5 10.1 convert_bitcast_fusion.1
  476.7 102.6 %reduce-scatter.16.cloned.1.call-done = f32[128,1,2048]{2,0,1:T(8,128)} async-done(((f32[2048,1,2048]{2,0,1:T(8,128)}), f32[128,1,2048]{2,0,1:T(8,128)}) %reduce-scatter.16.cloned.1.call-update) | async-done | bytes 1048592 | tf_op jit(solution)/shard_map/reduce_scatter | solution.py:227
  581.0 86.3 %reduce-scatter.14.cloned.1.call-done = bf16[128,1,2048]{2,0,1:T(8,128)(2,1)} async-done(((bf16[2048,1,2048]{2,0,1:T(8,128)(2,1)}), bf16[128,1,2048]{2,0,1:T(8,128)(2,1)}) %reduce-scatter.14.cloned.1.call-update) | async-done | bytes 524304 | tf_op jit(solution)/shard_map/reduce_scatter | solution.py:197
  680.2 61.5 %all-gather.8.cloned.1.call-done = bf16[2048,1,2048]{2,0,1:T(8,128)(2,1)} async-done(((bf16[128,1,2048]{2,0,1:T(8,128)(2,1)}), bf16[2048,1,2048]{2,0,1:T(8,128)(2,1)}) %all-gather.8.cloned.1.call-update) | async-done | bytes 8388624 | tf_op jit(solution)/shard_map/all_gather | solution.py:239
  741.7 5.7 fusion.37
  759.5 10.2 multiply_reduce_fusion
  769.7 9.4 multiply_convert_fusion.2
  796.0 9.7 convert_bitcast_fusion
  809.1 11.3 multiply_convert_fusion
  820.5 10.2 multiply_convert_fusion.1
  830.7 5.5 fusion.45
  836.5 8.4 fusion.30
  845.7 45.0 %reduce-scatter.18.cloned.1.call-done = bf16[128,1,2048]{2,0,1:T(8,128)(2,1)} async-done(((bf16[2048,1,2048]{2,0,1:T(8,128)(2,1)}), bf16[128,1,2048]{2,0,1:T(8,128)(2,1)}) %reduce-scatter.18.cloned.1.call-update) | async-done | bytes 524304 | tf_op jit(solution)/shard_map/reduce_scatter | solution.py:259
  898.3 84.3 %all-reduce = f32[8192]{0:T(1024)S(1)} all-reduce(f32[8192]{0:T(1024)S(1)} %broadcast_multiply_fusion.1), channel_id=10, replica_groups=mesh['group'=4,'dp'=2,'tensor'=16] {'group','dp','tensor'}, use_global_device_ids=true, to_apply=%region_38.39.clone | all-reduce | flops 8192 | bytes 65536
  985.0 27.6 %reduce-scatter.24.cloned.1.call-done = bf16[256,512]{1,0:T(8,128)(2,1)} async-done(((bf16[2048,512]{1,0:T(8,128)(2,1)}), bf16[256,512]{1,0:T(8,128)(2,1)}) %reduce-scatter.24.cloned.1.call-update) | async-done | bytes 262160 | tf_op jit(solution)/shard_map/reduce_scatter | solution.py:283
  1014.4 38.7 %reduce-scatter.22.cloned.1.call-done = bf16[1,128,256]{2,1,0:T(8,128)(2,1)} async-done(((bf16[1,128,2048]{2,1,0:T(8,128)(2,1)}), bf16[1,128,256]{2,1,0:T(8,128)(2,1)}) %reduce-scatter.22.cloned.1.call-update) | async-done | bytes 65552 | tf_op jit(solution)/shard_map/reduce_scatter | solution.py:280
  1054.6 45.8 %reduce-scatter.20.cloned.1.call-done = bf16[256,3,1,128]{3,0,1,2:T(8,128)(2,1)} async-done(((bf16[2048,3,1,128]{3,0,1,2:T(8,128)(2,1)}), bf16[256,3,1,128]{3,0,1,2:T(8,128)(2,1)}) %reduce-scatter.20.cloned.1.call-update) | async-done | bytes 196624 | tf_op jit(solution)/shard_map/reduce_scatter | solution.py:277
  1102.4 716.0 %reduce-scatter.28.cloned.1.call-done = f32[16,8]{1,0:T(8,128)} async-done(((f32[2048,8]{1,0:T(8,128)}), f32[16,8]{1,0:T(8,128)}) %reduce-scatter.28.cloned.1.call-update) | async-done | bytes 528
  (254 shorter events, 102.5 us)
Async XLA Ops:
  7.2 437.2 %copy-start = (bf16[512,2048]{1,0:T(8,128)(2,1)S(1)}, bf16[512,2048]{1,0:T(8,128)(2,1)}, u32[]{:S(2)}) copy-start(bf16[512,2048]{1,0:T(8,128)(2,1)} %param.28) | copy-start | bytes 6291460
  7.2 77.6 %all-gather.4.cloned.1.call-start = ((), (), s32[]{:S(2)}) async-start(), calls=%async_computation.10 | async-start | bytes 8912896 | tf_op jit(solution)/shard_map/all_gather | solution.py:141
  9.9 82.3 %copy-start.61 = (f32[128]{0:T(128)}, f32[128]{0:T(128)S(1)}, u32[]{:S(2)}) copy-start(f32[128]{0:T(128)S(1)} %fusion.73) | copy-start | bytes 1540
  12.8 234.8 %reduce-scatter.12.cloned.1.call-start = ((), (), s32[]{:S(2)}) async-start(), calls=%async_computation.11 | async-start | bytes 17825792 | tf_op jit(solution)/shard_map/reduce_scatter | solution.py:175
  16.0 741.7 %copy-start.36 = (s32[512]{0:T(512)}, s32[512]{0:T(512)S(1)}, u32[]{:S(2)}) copy-start(s32[512]{0:T(512)S(1)} %iota_add_fusion.2) | copy-start | bytes 6148
  16.0 741.7 %copy-start.34 = (s32[512]{0:T(512)}, s32[512]{0:T(512)S(1)}, u32[]{:S(2)}) copy-start(s32[512]{0:T(512)S(1)} %iota_add_fusion) | copy-start | bytes 6148
  137.2 110.3 %copy-start.47 = (f32[2048]{0:T(1024)S(1)}, f32[2048]{0:T(1024)}, u32[]{:S(2)}) copy-start(f32[2048]{0:T(1024)} %param.23) | copy-start | bytes 24580
  137.2 112.2 %copy-start.32 = (f32[2048]{0:T(1024)S(1)}, f32[2048]{0:T(1024)}, u32[]{:S(2)}) copy-start(f32[2048]{0:T(1024)} %param.24) | copy-start | bytes 24580
  137.2 112.2 %copy-start.48 = (f32[2048]{0:T(1024)S(1)}, f32[2048]{0:T(1024)}, u32[]{:S(2)}) copy-start(f32[2048]{0:T(1024)} %param.25) | copy-start | bytes 24580
  137.3 296.6 %all-gather.6.cloned.1.call-start = ((), (), s32[]{:S(2)}) async-start(), calls=%async_computation.12 | async-start | bytes 8912896 | tf_op jit(solution)/shard_map/all_gather | solution.py:185
  251.2 418.7 %copy-start.53 = (pred[128]{0:T(512)(128)(4,1)}, pred[128]{0:T(512)(128)(4,1)S(1)}, u32[]{:S(2)}) copy-start(pred[128]{0:T(512)(128)(4,1)S(1)} %add_compare_fusion) | copy-start | bytes 388
  256.6 187.8 %all-to-all-start = ((bf16[16,128,1,2048]{3,1,2,0:T(8,128)(2,1)}), bf16[16,128,1,2048]{3,1,2,0:T(8,128)(2,1)}, u32[]{:S(2)}, u32[]{:S(2)}) async-start(bf16[16,128,1,2048]{3,1,2,0:T(8,128)(2,1)} %stack.16), calls=%async_computation.2 | async-start | bytes 16777216 | tf_op jit(solution)/shard_map/all_to_all | solution.py:11
  261.9 182.5 %copy-start.64 = (f32[512]{0:T(512)S(1)}, f32[512]{0:T(512)}, u32[]{:S(2)}) copy-start(f32[512]{0:T(512)} %param.27) | copy-start | bytes 6148
  261.9 317.5 %reduce-scatter.16.cloned.1.call-start = ((), (), s32[]{:S(2)}) async-start(), calls=%async_computation.14 | async-start | bytes 17825792 | tf_op jit(solution)/shard_map/reduce_scatter | solution.py:227
  466.5 200.8 %reduce-scatter.14.cloned.1.call-start = ((), (), s32[]{:S(2)}) async-start(), calls=%async_computation.13 | async-start | bytes 8912896 | tf_op jit(solution)/shard_map/reduce_scatter | solution.py:197
  476.6 190.6 %copy-start.49 = (f32[2048]{0:T(1024)S(1)}, f32[2048]{0:T(1024)}, u32[]{:S(2)}) copy-start(f32[2048]{0:T(1024)} %param.29) | copy-start | bytes 24580
  476.7 193.2 %copy-start.15 = (bf16[128,1,2048]{2,0,1:T(8,128)(2,1)S(1)}, bf16[128,1,2048]{2,0,1:T(8,128)(2,1)}, u32[]{:S(2)}) copy-start(bf16[128,1,2048]{2,0,1:T(8,128)(2,1)} %param.16) | copy-start | bytes 1572868
  476.7 265.1 %all-gather.8.cloned.1.call-start = ((), (), s32[]{:S(2)}) async-start(), calls=%async_computation.15 | async-start | bytes 8912896 | tf_op jit(solution)/shard_map/all_gather | solution.py:239
  671.6 219.1 %reduce-scatter.18.cloned.1.call-start = ((), (), s32[]{:S(2)}) async-start(), calls=%async_computation.16 | async-start | bytes 8912896 | tf_op jit(solution)/shard_map/reduce_scatter | solution.py:259
  676.2 81.5 %copy-start.38 = (f32[512]{0:T(512)}, f32[512]{0:T(512)S(1)}, u32[]{:S(2)}) copy-start(f32[512]{0:T(512)S(1)} %get-tuple-element.150) | copy-start | bytes 6148
  676.2 81.5 %copy-start.40 = (f32[512]{0:T(512)}, f32[512]{0:T(512)S(1)}, u32[]{:S(2)}) copy-start(f32[512]{0:T(512)S(1)} %get-tuple-element.149) | copy-start | bytes 6148
  676.8 65.0 %copy-start.30 = (bf16[1,128,2048]{2,1,0:T(8,128)(2,1)S(1)}, bf16[1,128,2048]{2,1,0:T(8,128)(2,1)}, u32[]{:S(2)}) copy-start(bf16[1,128,2048]{2,1,0:T(8,128)(2,1)} %param.22) | copy-start | bytes 1572868
  678.9 78.8 %copy-start.42 = (f32[512]{0:T(512)}, f32[512]{0:T(512)S(1)}, u32[]{:S(2)}) copy-start(f32[512]{0:T(512)S(1)} %get-tuple-element.151) | copy-start | bytes 6148
  678.9 78.8 %copy-start.44 = (f32[512]{0:T(512)}, f32[512]{0:T(512)S(1)}, u32[]{:S(2)}) copy-start(f32[512]{0:T(512)S(1)} %get-tuple-element.152) | copy-start | bytes 6148
  805.7 177.5 %reduce-scatter.26.cloned.1.call-start = ((), (), s32[]{:S(2)}) async-start(), calls=%async_computation.20 | async-start | bytes 2359296 | tf_op jit(solution)/shard_map/reduce_scatter | solution.py:286
  820.4 192.2 %reduce-scatter.24.cloned.1.call-start = ((), (), s32[]{:S(2)}) async-start(), calls=%async_computation.19 | async-start | bytes 2359296 | tf_op jit(solution)/shard_map/reduce_scatter | solution.py:283
  830.6 222.5 %reduce-scatter.22.cloned.1.call-start = ((), (), s32[]{:S(2)}) async-start(), calls=%async_computation.18 | async-start | bytes 589824 | tf_op jit(solution)/shard_map/reduce_scatter | solution.py:280
  836.3 55.9 %copy-start.62 = (f32[128]{0:T(128)S(1)}, f32[128]{0:T(128)}, u32[]{:S(2)}) copy-start(f32[128]{0:T(128)} %copy-done.61) | copy-start | bytes 1540
  836.3 55.9 %copy-start.52 = (f32[128]{0:T(128)S(1)}, f32[128]{0:T(128)}, u32[]{:S(2)}) copy-start(f32[128]{0:T(128)} %copy-done.51) | copy-start | bytes 1540
  836.3 264.1 %reduce-scatter.20.cloned.1.call-start = ((), (), s32[]{:S(2)}) async-start(), calls=%async_computation.17 | async-start | bytes 1769472 | tf_op jit(solution)/shard_map/reduce_scatter | solution.py:277
  845.0 973.4 %reduce-scatter.28.cloned.1.call-start = ((), (), s32[]{:S(2)}) async-start(), calls=%async_computation.21 | async-start | bytes 1056768
  892.2 932.1 %copy-start.1 = (bf16[512,2048]{1,0:T(8,128)(2,1)S(1)}, bf16[512,2048]{1,0:T(8,128)(2,1)}, u32[]{:S(2)}) copy-start(bf16[512,2048]{1,0:T(8,128)(2,1)} %param.28) | copy-start | bytes 6291460
  (49 other events, 633.2 us)
Sparse Core Ops, SparseCore 0:
  12.9 71.8 all-gather.3
  137.4 110.1 reduce-scatter.11
  250.6 183.1 all-gather.5
  466.6 112.7 reduce-scatter.15
  582.6 84.6 reduce-scatter.13
  671.7 70.0 all-gather.7
  805.8 84.8 reduce-scatter.17
  893.1 55.0 reduce-scatter.25
  950.6 61.8 reduce-scatter.23
  1014.8 38.2 reduce-scatter.21
  1055.6 44.7 reduce-scatter.19
  1102.8 715.5 reduce-scatter.27
